TPU v7x, 32 devices: a whole 2x2x4 slice. The times are simulated.
32 devices in a mesh: dp: 4 (over x, core), fsdp: 2 (over y), tensor: 4 (over z).
Axes of the slice: x: 2, y: 2, z: 4, core: 2. Of those that a mesh axis runs over, the one named last changes fastest.
Arguments:
- layer_input: bfloat16 [4096, 2048], P(('dp', 'fsdp', 'tensor')), may hold values from -6 to 6
- first_gain: bfloat16 [2048], P('fsdp'), may hold values from 0.5 to 1.5
- w_query: bfloat16 [2048, 2048], P('fsdp', 'tensor'), may hold values from -0.125 to 0.125
- w_key: bfloat16 [2048, 2048], P('fsdp', 'tensor'), may hold values from -0.125 to 0.125
- w_value: bfloat16 [2048, 2048], P('fsdp', 'tensor'), may hold values from -0.125 to 0.125
- w_gating: bfloat16 [2048, 2048], P('fsdp', 'tensor'), may hold values from -0.125 to 0.125
- w_beta: bfloat16 [2048, 16], P('fsdp', 'tensor'), may hold values from -0.125 to 0.125
- conv_query: bfloat16 [4, 2048], P(None, 'tensor'), may hold values from -3 to 3
- conv_key: bfloat16 [4, 2048], P(None, 'tensor'), may hold values from -3 to 3
- conv_value: bfloat16 [4, 2048], P(None, 'tensor'), may hold values from -3 to 3
- head_gain: bfloat16 [128], replicated, may hold values from 0.5 to 1.5
- w_project: bfloat16 [2048, 2048], P('tensor', 'fsdp'), may hold values from -0.1875 to 0.1875
- second_gain: bfloat16 [2048], P('fsdp'), may hold values from 0.5 to 1.5
- w_gate: bfloat16 [2048, 5632], P('fsdp', 'tensor'), may hold values from -0.125 to 0.125
- w_up: bfloat16 [2048, 5632], P('fsdp', 'tensor'), may hold values from -0.125 to 0.125
- w_down: bfloat16 [5632, 2048], P('tensor', 'fsdp'), may hold values from -0.109375 to 0.109375
- doc_starts: int32 [8, 4], P(('dp', 'fsdp')), may hold values from 1 to 508, as said below
- seq_lengths: int32 [8], P(('dp', 'fsdp')), may hold values from 256 to 512, as said below
- output_grad: bfloat16 [4096, 2048], P(('dp', 'fsdp', 'tensor')), may hold values from -6 to 6
Outputs:
- result: bfloat16 [4096, 2048], P(('dp', 'fsdp', 'tensor'))
- input_grad: float32 [4096, 2048], P(('dp', 'fsdp', 'tensor'))
- grad_first: float32 [2048], P(('dp', 'fsdp'))
- grad_query: float32 [2048, 2048], P(('dp', 'fsdp'), 'tensor')
- grad_key: float32 [2048, 2048], P(('dp', 'fsdp'), 'tensor')
- grad_value: float32 [2048, 2048], P(('dp', 'fsdp'), 'tensor')
- grad_gating: float32 [2048, 2048], P(('dp', 'fsdp'), 'tensor')
- grad_beta: float32 [2048, 16], P(('dp', 'fsdp'), 'tensor')
- convgrad_query: float32 [4, 2048], P(None, 'tensor')
- convgrad_key: float32 [4, 2048], P(None, 'tensor')
- convgrad_value: float32 [4, 2048], P(None, 'tensor')
- grad_head: float32 [128], replicated
- grad_project: float32 [2048, 2048], P('tensor', ('dp', 'fsdp'))
- grad_second: float32 [2048], P(('dp', 'fsdp'))
- grad_gate: float32 [2048, 5632], P(('dp', 'fsdp'), 'tensor')
- grad_up: float32 [2048, 5632], P(('dp', 'fsdp'), 'tensor')
- grad_down: float32 [5632, 2048], P('tensor', ('dp', 'fsdp'))
Inputs may be any that keep to these rules, and one draw needn't show every extreme that they name: `doc_starts`: each row rises strictly; position 0 begins the first document of a sequence and each entry begins the next. `seq_lengths`: rows at positions at or past a sequence's length are padding.
All inputs are finite; a program needn't handle non-finite values.
Results may differ from a plain program's by a relative error of at most 0.015.
Values may be sent and summed in bfloat16 or wider, within the bound.
A program may use at most 256 MiB of HBM per device.

v0:
```python
import jax
import jax.numpy as jnp
from jax import lax
from jax.sharding import PartitionSpec as P

KERNEL = 4
BLOCK = 64


def rms_scale(values):
    return lax.rsqrt(jnp.mean(values * values, axis=-1, keepdims=True) + 1e-05)


def rms_back(values, scale_rows, gain, grad):
    scaled_grad = grad * gain
    inner = jnp.mean(scaled_grad * values, axis=-1, keepdims=True)
    return scale_rows * (scaled_grad - values * scale_rows * scale_rows * inner)


def short_conv(raw_rows, weights, doc_ids):
    row_count = raw_rows.shape[0]
    total = jnp.zeros_like(raw_rows)
    for tap_index in range(KERNEL):
        delay_rows = KERNEL - 1 - tap_index
        moved = jnp.pad(raw_rows, ((delay_rows, 0), (0, 0)))[:row_count]
        moved_doc = jnp.pad(doc_ids, (delay_rows, 0), constant_values=-1)[:row_count]
        keep_mask = (moved_doc == doc_ids).astype(raw_rows.dtype)
        total = total + weights[tap_index] * moved * keep_mask[:, None]
    return total


def delta_rule(query, keyed, valued, rate, doc_ids):
    row_count, head_count, head_width = query.shape
    blocks = row_count // BLOCK
    float_type = query.dtype

    def to_blocks(array):
        return array.reshape(blocks, BLOCK, head_count, head_width).transpose(0, 2, 1, 3)

    query_blk = to_blocks(query)
    key_blk = to_blocks(keyed)
    value_blk = to_blocks(valued)
    rate_blk = rate.reshape(blocks, BLOCK, head_count).transpose(0, 2, 1)
    doc_blk = doc_ids.reshape(blocks, BLOCK)
    prior_doc = jnp.concatenate([jnp.full((1,), -1, jnp.int32), doc_blk[:-1, -1]])
    carry_in = (doc_blk == prior_doc[:, None]).astype(float_type)
    same_doc = doc_blk[:, :, None] == doc_blk[:, None, :]
    positions = jnp.arange(BLOCK)
    strict = positions[:, None] > positions[None, :]
    inclusive = positions[:, None] >= positions[None, :]
    key_key = jnp.einsum("nhtd,nhsd->nhts", key_blk, key_blk, precision=lax.Precision.HIGHEST)
    mixing = key_key * rate_blk[..., None] * (same_doc & strict)[:, None].astype(float_type)
    system = mixing + jnp.eye(BLOCK, dtype=float_type)
    scaled_values = value_blk * rate_blk[..., None]
    scaled_keys = key_blk * (rate_blk * carry_in[:, None, :])[..., None]
    solved_values = jax.scipy.linalg.solve_triangular(
        system, scaled_values, lower=True, unit_diagonal=True
    )
    solved_keys = jax.scipy.linalg.solve_triangular(
        system, scaled_keys, lower=True, unit_diagonal=True
    )
    scores = jnp.einsum("nhtd,nhsd->nhts", query_blk, key_blk, precision=lax.Precision.HIGHEST)
    scores = scores * (same_doc & inclusive)[:, None].astype(float_type)
    last_same = (doc_blk == doc_blk[:, -1:]).astype(float_type)
    carry_end = carry_in[:, -1]

    def advance(memory, inputs):
        solved_v, solved_k, score_n, query_n, key_n, carry_n, last_n, end_n = inputs
        update = solved_v - jnp.einsum(
            "htk,hvk->htv", solved_k, memory, precision=lax.Precision.HIGHEST
        )
        output = carry_n[None, :, None] * jnp.einsum(
            "hvk,htk->htv", memory, query_n, precision=lax.Precision.HIGHEST
        )
        output = output + jnp.einsum(
            "hts,hsv->htv", score_n, update, precision=lax.Precision.HIGHEST
        )
        memory = end_n * memory + jnp.einsum(
            "htv,htk->hvk", update * last_n[None, :, None], key_n, precision=lax.Precision.HIGHEST
        )
        return (memory, output)

    initial = jnp.zeros((head_count, head_width, head_width), float_type)
    _, outputs = lax.scan(
        advance,
        initial,
        (solved_values, solved_keys, scores, query_blk, key_blk, carry_in, last_same, carry_end),
    )
    return outputs.transpose(0, 2, 1, 3).reshape(row_count, head_count, head_width)


def mixer(
    query_raw,
    key_raw,
    value_raw,
    gating_raw,
    beta_raw,
    conv_q,
    conv_k,
    conv_v,
    gain_head,
    doc_ids,
    live,
):
    head_width = gain_head.shape[0]
    row_count = query_raw.shape[0]
    query_unit = jax.nn.silu(short_conv(query_raw, conv_q, doc_ids)).reshape(
        row_count, -1, head_width
    )
    query_unit = query_unit * lax.rsqrt(
        jnp.sum(query_unit * query_unit, axis=-1, keepdims=True) + 1e-06
    )
    key_unit = jax.nn.silu(short_conv(key_raw, conv_k, doc_ids)).reshape(row_count, -1, head_width)
    key_unit = key_unit * lax.rsqrt(jnp.sum(key_unit * key_unit, axis=-1, keepdims=True) + 1e-06)
    value_rows = jax.nn.silu(short_conv(value_raw, conv_v, doc_ids)).reshape(
        row_count, -1, head_width
    )
    beta_rate = jax.nn.sigmoid(beta_raw) * live[:, None]
    mixed = delta_rule(query_unit, key_unit, value_rows, beta_rate, doc_ids)
    norm_scale = lax.rsqrt(jnp.mean(mixed * mixed, axis=-1, keepdims=True) + 1e-05)
    gated = (
        mixed * norm_scale * gain_head * jax.nn.silu(gating_raw.reshape(row_count, -1, head_width))
    )
    gated = gated * live[:, None, None]
    return gated.reshape(row_count, -1)


def matmul(left, right):
    return jnp.dot(left, right, preferred_element_type=jnp.float32)


def matmul_nt(left, right):
    return lax.dot_general(
        left, right, (((1,), (1,)), ((), ())), preferred_element_type=jnp.float32
    )


def matmul_tn(left, right):
    return lax.dot_general(
        left, right, (((0,), (0,)), ((), ())), preferred_element_type=jnp.float32
    )


def gather_rows(rows):
    return lax.all_gather(rows, "tensor", axis=0, tiled=True)


def scatter_rows(partial_rows):
    return lax.psum_scatter(partial_rows, "tensor", scatter_dimension=0, tiled=True)


def fetch_mixer(first_gain, w_query, w_key, w_value, w_gating, w_beta, w_project):
    return (
        lax.all_gather(first_gain, "fsdp", axis=0, tiled=True),
        lax.all_gather(w_query, "fsdp", axis=0, tiled=True),
        lax.all_gather(w_key, "fsdp", axis=0, tiled=True),
        lax.all_gather(w_value, "fsdp", axis=0, tiled=True),
        lax.all_gather(w_gating, "fsdp", axis=0, tiled=True),
        lax.all_gather(w_beta, "fsdp", axis=0, tiled=True),
        lax.all_gather(w_project, "fsdp", axis=1, tiled=True),
    )


def fetch_ffn(second_gain, w_gate, w_up, w_down):
    return (
        lax.all_gather(second_gain, "fsdp", axis=0, tiled=True),
        lax.all_gather(w_gate, "fsdp", axis=0, tiled=True),
        lax.all_gather(w_up, "fsdp", axis=0, tiled=True),
        lax.all_gather(w_down, "fsdp", axis=1, tiled=True),
    )


def body(
    layer_input,
    first_gain,
    w_query,
    w_key,
    w_value,
    w_gating,
    w_beta,
    conv_query,
    conv_key,
    conv_value,
    head_gain,
    w_project,
    second_gain,
    w_gate,
    w_up,
    w_down,
    doc_starts,
    seq_lengths,
    output_grad,
):
    input_float = layer_input.astype(jnp.float32)
    seq_rows = layer_input.shape[0] * lax.axis_size("tensor")
    positions = jnp.arange(seq_rows, dtype=jnp.int32)
    doc_ids = jnp.sum((doc_starts[0][None, :] <= positions[:, None]).astype(jnp.int32), axis=1)
    live = (positions < seq_lengths[0]).astype(jnp.float32)
    conv_q = conv_query.astype(jnp.float32)
    conv_k = conv_key.astype(jnp.float32)
    conv_v = conv_value.astype(jnp.float32)
    gain_head = head_gain.astype(jnp.float32)
    gain_one, query_full, key_full, value_full, gating_full, beta_full, project_full = fetch_mixer(
        first_gain, w_query, w_key, w_value, w_gating, w_beta, w_project
    )
    scale_one = rms_scale(input_float)
    normed1 = (input_float * scale_one * gain_one.astype(jnp.float32)).astype(jnp.bfloat16)
    rows_one = gather_rows(normed1)
    query_raw = matmul(rows_one, query_full)
    key_raw = matmul(rows_one, key_full)
    value_raw = matmul(rows_one, value_full)
    gating_raw = matmul(rows_one, gating_full)
    beta_raw = matmul(rows_one, beta_full)

    def mixer_local(
        query_in, key_in, value_in, gating_in, beta_in, conv_qin, conv_kin, conv_vin, gain_in
    ):
        return mixer(
            query_in,
            key_in,
            value_in,
            gating_in,
            beta_in,
            conv_qin,
            conv_kin,
            conv_vin,
            gain_in,
            doc_ids,
            live,
        )

    mixer_inputs = (
        query_raw,
        key_raw,
        value_raw,
        gating_raw,
        beta_raw,
        conv_q,
        conv_k,
        conv_v,
        gain_head,
    )
    gated_float, pullback = jax.vjp(mixer_local, *mixer_inputs)
    gated = gated_float.astype(jnp.bfloat16)
    attn_out = scatter_rows(matmul(gated, project_full))
    resid = input_float + attn_out
    gain_two, gate_full, up_full, down_full = fetch_ffn(second_gain, w_gate, w_up, w_down)
    scale_two = rms_scale(resid)
    normed2 = (resid * scale_two * gain_two.astype(jnp.float32)).astype(jnp.bfloat16)
    rows_two = gather_rows(normed2)
    gate_val = matmul(rows_two, gate_full)
    up_val = matmul(rows_two, up_full)
    gate_sig = jax.nn.sigmoid(gate_val)
    silu_gate = gate_val * gate_sig
    hidden = (silu_gate * up_val).astype(jnp.bfloat16)
    ffn_out = scatter_rows(matmul(hidden, down_full))
    result = (resid + ffn_out).astype(jnp.bfloat16)
    gain_two, gate_full, up_full, down_full = fetch_ffn(second_gain, w_gate, w_up, w_down)
    grad_rows = gather_rows(output_grad)
    d_hidden = matmul_nt(grad_rows, down_full)
    grad_down = matmul_tn(hidden, grad_rows)
    d_gate = (d_hidden * up_val * gate_sig * (1.0 + gate_val * (1.0 - gate_sig))).astype(
        jnp.bfloat16
    )
    d_up = (d_hidden * silu_gate).astype(jnp.bfloat16)
    grad_gate = matmul_tn(rows_two, d_gate)
    grad_up = matmul_tn(rows_two, d_up)
    d_normed2 = scatter_rows(matmul_nt(d_gate, gate_full) + matmul_nt(d_up, up_full))
    grad_second = jnp.sum(d_normed2 * resid * scale_two, axis=0)
    d_resid = output_grad.astype(jnp.float32) + rms_back(
        resid, scale_two, gain_two.astype(jnp.float32), d_normed2
    )
    gain_one, query_full, key_full, value_full, gating_full, beta_full, project_full = fetch_mixer(
        first_gain, w_query, w_key, w_value, w_gating, w_beta, w_project
    )
    d_attn = gather_rows(d_resid.astype(jnp.bfloat16))
    d_gated = matmul_nt(d_attn, project_full)
    grad_project = matmul_tn(gated, d_attn)
    cotangents = pullback(d_gated)
    d_query = cotangents[0].astype(jnp.bfloat16)
    d_key = cotangents[1].astype(jnp.bfloat16)
    d_value = cotangents[2].astype(jnp.bfloat16)
    d_gating = cotangents[3].astype(jnp.bfloat16)
    d_beta = cotangents[4].astype(jnp.bfloat16)
    grad_query = matmul_tn(rows_one, d_query)
    grad_key = matmul_tn(rows_one, d_key)
    grad_value = matmul_tn(rows_one, d_value)
    grad_gating = matmul_tn(rows_one, d_gating)
    grad_beta = matmul_tn(rows_one, d_beta)
    d_norm_one = (
        matmul_nt(d_query, query_full) + matmul_nt(d_key, key_full) + matmul_nt(d_value, value_full)
    )
    d_norm_one = d_norm_one + matmul_nt(d_gating, gating_full) + matmul_nt(d_beta, beta_full)
    d_normed1 = scatter_rows(d_norm_one)
    grad_first = jnp.sum(d_normed1 * input_float * scale_one, axis=0)
    input_grad = d_resid + rms_back(input_float, scale_one, gain_one.astype(jnp.float32), d_normed1)
    gain_totals = lax.psum((grad_first, grad_second, cotangents[8]), "tensor")
    conv_totals = lax.psum(
        (cotangents[5], cotangents[6], cotangents[7], gain_totals[2]), ("dp", "fsdp")
    )
    shards = (
        lax.psum_scatter(
            gain_totals[0].astype(jnp.bfloat16), ("dp", "fsdp"), scatter_dimension=0, tiled=True
        ).astype(jnp.float32),
        lax.psum_scatter(
            grad_query.astype(jnp.bfloat16), ("dp", "fsdp"), scatter_dimension=0, tiled=True
        ).astype(jnp.float32),
        lax.psum_scatter(
            grad_key.astype(jnp.bfloat16), ("dp", "fsdp"), scatter_dimension=0, tiled=True
        ).astype(jnp.float32),
        lax.psum_scatter(
            grad_value.astype(jnp.bfloat16), ("dp", "fsdp"), scatter_dimension=0, tiled=True
        ).astype(jnp.float32),
        lax.psum_scatter(
            grad_gating.astype(jnp.bfloat16), ("dp", "fsdp"), scatter_dimension=0, tiled=True
        ).astype(jnp.float32),
        lax.psum_scatter(
            grad_beta.astype(jnp.bfloat16), ("dp", "fsdp"), scatter_dimension=0, tiled=True
        ).astype(jnp.float32),
        lax.psum_scatter(
            grad_project.astype(jnp.bfloat16), ("dp", "fsdp"), scatter_dimension=1, tiled=True
        ).astype(jnp.float32),
        lax.psum_scatter(
            gain_totals[1].astype(jnp.bfloat16), ("dp", "fsdp"), scatter_dimension=0, tiled=True
        ).astype(jnp.float32),
        lax.psum_scatter(
            grad_gate.astype(jnp.bfloat16), ("dp", "fsdp"), scatter_dimension=0, tiled=True
        ).astype(jnp.float32),
        lax.psum_scatter(
            grad_up.astype(jnp.bfloat16), ("dp", "fsdp"), scatter_dimension=0, tiled=True
        ).astype(jnp.float32),
        lax.psum_scatter(
            grad_down.astype(jnp.bfloat16), ("dp", "fsdp"), scatter_dimension=1, tiled=True
        ).astype(jnp.float32),
    )
    return (
        result,
        input_grad,
        shards[0],
        shards[1],
        shards[2],
        shards[3],
        shards[4],
        shards[5],
        conv_totals[0],
        conv_totals[1],
        conv_totals[2],
        conv_totals[3],
        shards[6],
        shards[7],
        shards[8],
        shards[9],
        shards[10],
    )


def solution(mesh):
    placed = (
        P(("dp", "fsdp", "tensor"), None),
        P("fsdp"),
        P("fsdp", "tensor"),
        P("fsdp", "tensor"),
        P("fsdp", "tensor"),
        P("fsdp", "tensor"),
        P("fsdp", "tensor"),
        P(None, "tensor"),
        P(None, "tensor"),
        P(None, "tensor"),
        P(),
        P("tensor", "fsdp"),
        P("fsdp"),
        P("fsdp", "tensor"),
        P("fsdp", "tensor"),
        P("tensor", "fsdp"),
        P(("dp", "fsdp"), None),
        P(("dp", "fsdp")),
        P(("dp", "fsdp", "tensor"), None),
    )
    return jax.shard_map(
        body,
        mesh=mesh,
        in_specs=placed,
        out_specs=(
            P(("dp", "fsdp", "tensor"), None),
            P(("dp", "fsdp", "tensor"), None),
            P(("dp", "fsdp")),
            P(("dp", "fsdp"), "tensor"),
            P(("dp", "fsdp"), "tensor"),
            P(("dp", "fsdp"), "tensor"),
            P(("dp", "fsdp"), "tensor"),
            P(("dp", "fsdp"), "tensor"),
            P(None, "tensor"),
            P(None, "tensor"),
            P(None, "tensor"),
            P(),
            P("tensor", ("dp", "fsdp")),
            P(("dp", "fsdp")),
            P(("dp", "fsdp"), "tensor"),
            P(("dp", "fsdp"), "tensor"),
            P("tensor", ("dp", "fsdp")),
        ),
        check_vma=False,
    )
```

profile of v0, /device:TPU:0, one launch (start us, length us, event | category | flops | bytes accessed | tf_op | source)
XLA Modules:
  0.0 1605.7 jit_solution(16888827830021161958)
XLA Ops:
  26.4 19.2 %all-gather.19.cloned.1.call-done = bf16[2048,512]{1,0:T(8,128)(2,1)} async-done(((bf16[1024,512]{1,0:T(8,128)(2,1)}), bf16[2048,512]{1,0:T(8,128)(2,1)}) %all-gather.19.cloned.1.call-update) | async-done | bytes 2097168 | tf_op jit(solution)/shard_map/all_gather | solution.py:155
  45.6 48.2 %all-gather.13.cloned.1.call-done = bf16[512,2048]{1,0:T(8,128)(2,1)} async-done(((bf16[128,2048]{1,0:T(8,128)(2,1)}), bf16[512,2048]{1,0:T(8,128)(2,1)}) %all-gather.13.cloned.1.call-update) | async-done | bytes 2097168 | tf_op jit(solution)/shard_map/all_gather | solution.py:145
  98.4 28.8 %all-gather.17.cloned.1.call-done = bf16[2048,512]{1,0:T(8,128)(2,1)} async-done(((bf16[1024,512]{1,0:T(8,128)(2,1)}), bf16[2048,512]{1,0:T(8,128)(2,1)}) %all-gather.17.cloned.1.call-update) | async-done | bytes 2097168 | tf_op jit(solution)/shard_map/all_gather | solution.py:157
  136.1 25.6 %all-gather.15.cloned.1.call-done = bf16[2048,512]{1,0:T(8,128)(2,1)} async-done(((bf16[1024,512]{1,0:T(8,128)(2,1)}), bf16[2048,512]{1,0:T(8,128)(2,1)}) %all-gather.15.cloned.1.call-update) | async-done | bytes 2097168 | tf_op jit(solution)/shard_map/all_gather | solution.py:156
  182.0 158.2 %custom-call.12 = f32[8,4,1,64,64]{3,4,2,1,0:T(8,128)S(1)} custom-call(f32[8,4,1,64,64]{4,3,2,1,0:T(8,128)} %add_bitcast_fusion), custom_call_target="InvertDiagBlocksLowerTriangular" | custom-call | tf_op jit(solution)/shard_map/jvp(jit(_solve_triangular))/vmap(vmap())/triangular_solve | solution.py:56
  356.3 70.5 %while.48 = (s32[]{:T(128)}, f32[4,128,128]{2,1,0:T(8,128)S(1)}, f32[8,4,64,128]{3,2,1,0:T(8,128)}, f32[8,4,128,128]{3,2,1,0:T(8,128)}, f32[8,1,64,1]{2,3,1,0:T(...) while((s32[]{:T(128)}, f32[4,128,128]{2,1,0:T(8,128)S(1)}, ...), condition=%wide.region_5.7_spmd.clone, body=%wide.region_4.6_spmd.clone.sunk | while | flops 176717824 | bytes 3283676 | solution.py:84
  447.0 71.4 %reduce-scatter.16.cloned.1.call-done = f32[128,2048]{1,0:T(8,128)} async-done(((f32[512,2048]{1,0:T(8,128)}), f32[128,2048]{1,0:T(8,128)}) %reduce-scatter.16.cloned.1.call-update) | async-done | bytes 1048592 | tf_op jit(solution)/shard_map/reduce_scatter | solution.py:149
  522.9 72.1 %all-gather.27.cloned.1.call-done = bf16[2048,1408]{1,0:T(8,128)(2,1)} async-done(((bf16[1024,1408]{1,0:T(8,128)(2,1)}), bf16[2048,1408]{1,0:T(8,128)(2,1)}) %all-gather.27.cloned.1.call-update) | async-done | bytes 5767184 | tf_op jit(solution)/shard_map/all_gather | solution.py:167
  595.0 48.2 %all-gather.25.cloned.1.call-done = bf16[512,2048]{1,0:T(8,128)(2,1)} async-done(((bf16[128,2048]{1,0:T(8,128)(2,1)}), bf16[512,2048]{1,0:T(8,128)(2,1)}) %all-gather.25.cloned.1.call-update) | async-done | bytes 2097168 | tf_op jit(solution)/shard_map/all_gather | solution.py:145
  651.4 66.4 %all-gather.29.cloned.1.call-done = bf16[2048,1408]{1,0:T(8,128)(2,1)} async-done(((bf16[1024,1408]{1,0:T(8,128)(2,1)}), bf16[2048,1408]{1,0:T(8,128)(2,1)}) %all-gather.29.cloned.1.call-update) | async-done | bytes 5767184 | tf_op jit(solution)/shard_map/all_gather | solution.py:168
  726.2 39.3 %all-gather.33.cloned.1.call-done = bf16[512,2048]{1,0:T(8,128)(2,1)} async-done(((bf16[128,2048]{1,0:T(8,128)(2,1)}), bf16[512,2048]{1,0:T(8,128)(2,1)}) %all-gather.33.cloned.1.call-update) | async-done | bytes 2097168 | tf_op jit(solution)/shard_map/all_gather | solution.py:145
  765.5 74.7 %all-gather.31.cloned.1.call-done = bf16[1408,2048]{1,0:T(8,128)(2,1)} async-done(((bf16[1408,1024]{1,0:T(8,128)(2,1)}), bf16[1408,2048]{1,0:T(8,128)(2,1)}) %all-gather.31.cloned.1.call-update) | async-done | bytes 5767184 | tf_op jit(solution)/shard_map/all_gather | solution.py:169
  862.3 76.9 %reduce-scatter.20.cloned.1.call-done = f32[128,2048]{1,0:T(8,128)} async-done(((f32[512,2048]{1,0:T(8,128)}), f32[128,2048]{1,0:T(8,128)}) %reduce-scatter.20.cloned.1.call-update) | async-done | bytes 1048592 | tf_op jit(solution)/shard_map/reduce_scatter | solution.py:149
  971.1 17.5 %all-gather.35.cloned.1.call-done = bf16[512,2048]{1,0:T(8,128)(2,1)} async-done(((bf16[128,2048]{1,0:T(8,128)(2,1)}), bf16[512,2048]{1,0:T(8,128)(2,1)}) %all-gather.35.cloned.1.call-update) | async-done | bytes 2097168 | tf_op jit(solution)/shard_map/all_gather | solution.py:145
  1007.6 126.0 %while.49 = (s32[]{:T(128)}, f32[4,128,128]{2,1,0:T(8,128)S(1)}, f32[8,4,64,128]{3,2,1,0:T(8,128)}, f32[8,4,64,128]{3,2,1,0:T(8,128)}, f32[8,4,64,64]{3,2,1,0:T(...) while((s32[]{:T(128)}, f32[4,128,128]{2,1,0:T(8,128)S(1)}, ...), condition=%wide.region_14.16_spmd.clone, body=%wide.region_13.15_spmd.clone.sunk | while | flops 352911360 | bytes 4731118 | solution.py:84
  1236.4 21.0 %reduce-scatter.24.cloned.1.call-done = bf16[256,512]{1,0:T(8,128)(2,1)} async-done(((bf16[2048,512]{1,0:T(8,128)(2,1)}), bf16[256,512]{1,0:T(8,128)(2,1)}) %reduce-scatter.24.cloned.1.call-update) | async-done | bytes 262160 | tf_op jit(solution)/shard_map/reduce_scatter | solution.py:305
  1259.2 43.0 %reduce-scatter.26.cloned.1.call-done = bf16[256,512]{1,0:T(8,128)(2,1)} async-done(((bf16[2048,512]{1,0:T(8,128)(2,1)}), bf16[256,512]{1,0:T(8,128)(2,1)}) %reduce-scatter.26.cloned.1.call-update) | async-done | bytes 262160 | tf_op jit(solution)/shard_map/reduce_scatter | solution.py:308
  1304.0 42.7 %reduce-scatter.28.cloned.1.call-done = bf16[256,512]{1,0:T(8,128)(2,1)} async-done(((bf16[2048,512]{1,0:T(8,128)(2,1)}), bf16[256,512]{1,0:T(8,128)(2,1)}) %reduce-scatter.28.cloned.1.call-update) | async-done | bytes 262160 | tf_op jit(solution)/shard_map/reduce_scatter | solution.py:311
  1348.5 43.1 %reduce-scatter.30.cloned.1.call-done = bf16[256,512]{1,0:T(8,128)(2,1)} async-done(((bf16[2048,512]{1,0:T(8,128)(2,1)}), bf16[256,512]{1,0:T(8,128)(2,1)}) %reduce-scatter.30.cloned.1.call-update) | async-done | bytes 262160 | tf_op jit(solution)/shard_map/reduce_scatter | solution.py:314
  1393.4 42.8 %reduce-scatter.32.cloned.1.call-done = bf16[512,256]{1,0:T(8,128)(2,1)} async-done(((bf16[512,2048]{1,0:T(8,128)(2,1)}), bf16[512,256]{1,0:T(8,128)(2,1)}) %reduce-scatter.32.cloned.1.call-update) | async-done | bytes 262160 | tf_op jit(solution)/shard_map/reduce_scatter | solution.py:320
  1438.0 77.3 %reduce-scatter.22.cloned.1.call-done = f32[128,2048]{1,0:T(8,128)} async-done(((f32[512,2048]{1,0:T(8,128)}), f32[128,2048]{1,0:T(8,128)}) %reduce-scatter.22.cloned.1.call-update) | async-done | bytes 1048592 | tf_op jit(solution)/shard_map/reduce_scatter | solution.py:149
  1516.7 18.8 %all-reduce.36 = (bf16[2048]{0:T(1024)(128)(2,1)S(1)}, f32[128]{0:T(128)S(1)}, bf16[2048]{0:T(1024)(128)(2,1)S(1)}) all-reduce(f32[2048]{0:T(1024)S(1)} %get-tuple-element.717, f32[128]{0:T(128)S(1)} %copy-done.107, f32[2048]{0:T(1024)S(1)} %get-tuple-element.701), channel_id=1, replica_groups=mesh['dp'=4,'fsdp'=2,'tensor'=4] {'tensor'}, use_global_device_ids=true, to_apply=%region_23.26 | all-reduce | flops 4224 | bytes 25600 | tf_op jit(solution)/shard_map/psum | solution.py:297
  1550.2 24.6 %all-reduce.35 = (f32[4,512]{1,0:T(4,128)}, f32[4,512]{1,0:T(4,128)}, f32[4,512]{1,0:T(4,128)}, f32[128]{0:T(128)}) all-reduce(f32[4,512]{1,0:T(4,128)S(1)} %pad_add_fusion.2, f32[4,512]{1,0:T(4,128)S(1)} %pad_add_fusion.1, f32[4,512]{1,0:T(4,128)S(1)} %pad_add_fusion, ...), channel_id=1, replica_groups=mesh['dp'=4,'fsdp'=2,'tensor'=4] {'dp','fsdp'}, use_global_device_ids=true, to_apply=%region_34.37 | all-reduce | flops 6272 | bytes 50176 | tf_op jit(solution)/shard_map/psum | solution.py:298
  1576.1 19.3 %reduce-scatter.18.cloned.1.call-done = f32[128,2048]{1,0:T(8,128)} async-done(((f32[512,2048]{1,0:T(8,128)}), f32[128,2048]{1,0:T(8,128)}) %reduce-scatter.18.cloned.1.call-update) | async-done | bytes 1048592 | tf_op jit(solution)/shard_map/reduce_scatter | solution.py:149
  (604 shorter events, 508.4 us)
Async XLA Ops:
  7.9 85.8 %all-gather.13.cloned.1.call-start = ((), (), s32[]{:S(2)}) async-start(), calls=%async_computation.13 | async-start | bytes 2621440 | tf_op jit(solution)/shard_map/all_gather | solution.py:145
  16.8 110.4 %all-gather.17.cloned.1.call-start = ((), (), s32[]{:S(2)}) async-start(), calls=%async_computation.15 | async-start | bytes 3145728 | tf_op jit(solution)/shard_map/all_gather | solution.py:157
  17.5 144.2 %all-gather.15.cloned.1.call-start = ((), (), s32[]{:S(2)}) async-start(), calls=%async_computation.14 | async-start | bytes 3145728 | tf_op jit(solution)/shard_map/all_gather | solution.py:156
  18.1 412.2 %all-gather.21.cloned.1.call-start = ((), (), s32[]{:S(2)}) async-start(), calls=%async_computation.17 | async-start | bytes 3145728 | tf_op jit(solution)/shard_map/all_gather | solution.py:158
  18.7 417.6 %all-gather.23.cloned.1.call-start = ((), (), s32[]{:S(2)}) async-start(), calls=%async_computation.18 | async-start | bytes 3145728 | tf_op jit(solution)/shard_map/all_gather | solution.py:160
  19.3 499.0 %reduce-scatter.16.cloned.1.call-start = ((), (), s32[]{:S(2)}) async-start(), calls=%async_computation.19 | async-start | bytes 5242880 | tf_op jit(solution)/shard_map/reduce_scatter | solution.py:149
  441.4 153.6 %all-gather.27.cloned.1.call-start = ((), (), s32[]{:S(2)}) async-start(), calls=%async_computation.21 | async-start | bytes 8650752 | tf_op jit(solution)/shard_map/all_gather | solution.py:167
  442.1 201.1 %all-gather.25.cloned.1.call-start = ((), (), s32[]{:S(2)}) async-start(), calls=%async_computation.20 | async-start | bytes 2621440 | tf_op jit(solution)/shard_map/all_gather | solution.py:145
  520.9 196.9 %all-gather.29.cloned.1.call-start = ((), (), s32[]{:S(2)}) async-start(), calls=%async_computation.22 | async-start | bytes 8650752 | tf_op jit(solution)/shard_map/all_gather | solution.py:168
  521.5 244.0 %all-gather.33.cloned.1.call-start = ((), (), s32[]{:S(2)}) async-start(), calls=%async_computation.25 | async-start | bytes 2621440 | tf_op jit(solution)/shard_map/all_gather | solution.py:145
  522.2 317.9 %all-gather.31.cloned.1.call-start = ((), (), s32[]{:S(2)}) async-start(), calls=%async_computation.23 | async-start | bytes 8650752 | tf_op jit(solution)/shard_map/all_gather | solution.py:169
  522.8 416.4 %reduce-scatter.20.cloned.1.call-start = ((), (), s32[]{:S(2)}) async-start(), calls=%async_computation.26 | async-start | bytes 5242880 | tf_op jit(solution)/shard_map/reduce_scatter | solution.py:149
  862.3 126.4 %all-gather.35.cloned.1.call-start = ((), (), s32[]{:S(2)}) async-start(), calls=%async_computation.27 | async-start | bytes 2621440 | tf_op jit(solution)/shard_map/all_gather | solution.py:145
  942.1 285.7 %reduce-scatter.34.cloned.1.call-start = ((), (), s32[]{:S(2)}) async-start(), calls=%async_computation.34 | async-start | bytes 6488064 | tf_op jit(solution)/shard_map/reduce_scatter | solution.py:326
  950.2 279.9 %reduce-scatter.36.cloned.1.call-start = ((), (), s32[]{:S(2)}) async-start(), calls=%async_computation.35 | async-start | bytes 6488064 | tf_op jit(solution)/shard_map/reduce_scatter | solution.py:329
  958.4 274.0 %reduce-scatter.38.cloned.1.call-start = ((), (), s32[]{:S(2)}) async-start(), calls=%async_computation.36 | async-start | bytes 6488064 | tf_op jit(solution)/shard_map/reduce_scatter | solution.py:332
  971.1 263.7 %reduce-scatter.40.cloned.1.call-start = ((), (), s32[]{:S(2)}) async-start(), calls=%async_computation.37 | async-start | bytes 589824
  1164.3 93.1 %reduce-scatter.24.cloned.1.call-start = ((), (), s32[]{:S(2)}) async-start(), calls=%async_computation.29 | async-start | bytes 2359296 | tf_op jit(solution)/shard_map/reduce_scatter | solution.py:305
  1180.8 121.4 %reduce-scatter.26.cloned.1.call-start = ((), (), s32[]{:S(2)}) async-start(), calls=%async_computation.30 | async-start | bytes 2359296 | tf_op jit(solution)/shard_map/reduce_scatter | solution.py:308
  1187.4 159.3 %reduce-scatter.28.cloned.1.call-start = ((), (), s32[]{:S(2)}) async-start(), calls=%async_computation.31 | async-start | bytes 2359296 | tf_op jit(solution)/shard_map/reduce_scatter | solution.py:311
  1194.3 197.3 %reduce-scatter.30.cloned.1.call-start = ((), (), s32[]{:S(2)}) async-start(), calls=%async_computation.32 | async-start | bytes 2359296 | tf_op jit(solution)/shard_map/reduce_scatter | solution.py:314
  1199.6 236.6 %reduce-scatter.32.cloned.1.call-start = ((), (), s32[]{:S(2)}) async-start(), calls=%async_computation.33 | async-start | bytes 2359296 | tf_op jit(solution)/shard_map/reduce_scatter | solution.py:320
  1204.8 310.4 %reduce-scatter.22.cloned.1.call-start = ((), (), s32[]{:S(2)}) async-start(), calls=%async_computation.28 | async-start | bytes 5242880 | tf_op jit(solution)/shard_map/reduce_scatter | solution.py:149
  1217.0 378.5 %reduce-scatter.18.cloned.1.call-start = ((), (), s32[]{:S(2)}) async-start(), calls=%async_computation.24 | async-start | bytes 5242880 | tf_op jit(solution)/shard_map/reduce_scatter | solution.py:149
  (118 other events, 5868.5 us)
Sparse Core Ops, SparseCore 0:
  9.6 35.9 all-gather.18
  47.7 45.9 all-gather.12
  128.6 33.1 all-gather.14
  163.1 33.1 all-gather.20
  197.7 33.2 all-gather.22
  441.5 76.8 reduce-scatter.15
  520.0 74.9 all-gather.26
  597.2 45.9 all-gather.24
  644.6 73.1 all-gather.28
  719.5 45.9 all-gather.32
  767.0 73.1 all-gather.30
  862.4 76.7 reduce-scatter.19
  942.2 46.4 all-gather.34
  992.0 57.7 reduce-scatter.33
  1053.4 59.0 reduce-scatter.35
  1115.8 59.0 reduce-scatter.37
  1178.7 34.0 reduce-scatter.39
  1216.1 41.2 reduce-scatter.23
  1260.9 41.2 reduce-scatter.25
  1305.5 41.2 reduce-scatter.27
  1350.4 41.2 reduce-scatter.29
  1394.9 41.2 reduce-scatter.31
  1438.4 76.7 reduce-scatter.21
  1517.5 77.8 reduce-scatter.17
  (1 shorter events, 31.8 us)
where the time goes:
time: 1620 us; the launch traced here: 1610 us
  waiting for transfers between devices  883 us (55%)
  matrix products  329 us (20%)
  other arithmetic  228 us (14%)
  local copies, waits for them, and re-layouts  73.6 us (5%)
  blocking collectives  72.9 us (5%)
  between operations  17.5 us (1%)
    reduce_scatter x4, waiting for transfers between devices, scatter_rows(): lax.psum_scatter(partial_rows, 'tensor', scatter_dimension=0, tiled=True)  245 us
    another operation x5, other arithmetic, delta_rule(): jax.scipy.linalg.solve_triangular(system, scaled_values, lower=True, unit...  160 us
    all_gather x4, waiting for transfers between devices, gather_rows(): return lax.all_gather(rows, 'tensor', axis=0, tiled=True)  153 us
    all_gather x1, waiting for transfers between devices, fetch_ffn(): lax.all_gather(w_down, 'fsdp', axis=1, tiled=True)  74.7 us
    all_gather x1, waiting for transfers between devices, fetch_ffn(): lax.all_gather(w_gate, 'fsdp', axis=0, tiled=True)  72.1 us
    all_gather x1, waiting for transfers between devices, fetch_ffn(): lax.all_gather(w_up, 'fsdp', axis=0, tiled=True)  66.4 us
    dot_general x24, matrix products, advance(): jnp.einsum('hvk,htk->htv', memory, query_n, precision=lax.Precision.HIGHEST)  52.5 us
    dot_general x9, matrix products, matmul(): return jnp.dot(left, right, preferred_element_type=jnp.float32)  47.9 us
  transfers between devices with their start and end apart: 25, of which 19 were waited for; matrix products, arithmetic and copies ran while one was open for 36% of the time, Pallas kernels for 0%

commit v1 on v0

--- a/solution.py
+++ b/solution.py
@@ -2,6 +2,7 @@
 import jax.numpy as jnp
 from jax import lax
 from jax.sharding import PartitionSpec as P
+from jax.lax import axis_index, axis_size, ppermute
 
 KERNEL = 4
 BLOCK = 64
@@ -142,7 +143,21 @@
 
 
 def gather_rows(rows):
-    return lax.all_gather(rows, "tensor", axis=0, tiled=True)
+
+    def settle_surface_all(vals, axis_name, dim_no):
+        long_array, h_now = (axis_size(axis_name), axis_index(axis_name))
+        inter, local_next = (vals, 1)
+        while local_next < long_array:
+            a_next = ppermute(
+                inter, axis_name, perm=list(map(lambda c: (c, c ^ local_next), range(long_array)))
+            )
+            kept_arr = jnp.concatenate([inter, a_next], axis=dim_no)
+            all_values = jnp.concatenate([a_next, inter], axis=dim_no)
+            inter = jnp.where(h_now & local_next == 0, kept_arr, all_values)
+            local_next = 2 * local_next
+        return inter
+
+    return settle_surface_all(rows, "tensor", 0)
 
 
 def scatter_rows(partial_rows):

time: 1620 us -> 1480 us (0.914)
  waiting for transfers between devices: 883 us -> 716 us
  starting transfers between devices: 1.44 us -> 17.9 us
    all_gather x4 -> x0, waiting for transfers between devices: 153 us -> none  [gather_rows(): return lax.all_gather(rows, 'tensor', axis=0, tiled=True)]
    ppermute x0 -> x8, waiting for transfers between devices: none -> 148 us  [settle_surface_all(): ppermute(inter, axis_name, perm=list(map(lambda c: (c, c ^ local_next), r...]
    all_gather x1, waiting for transfers between devices: 72.1 us -> 20.5 us  [fetch_ffn(): lax.all_gather(w_gate, 'fsdp', axis=0, tiled=True)]
    all_gather x1, waiting for transfers between devices: 28.8 us -> 0.01 us  [fetch_mixer(): lax.all_gather(w_value, 'fsdp', axis=0, tiled=True)]
    reduce_scatter x4, waiting for transfers between devices: 245 us -> 225 us  [scatter_rows(): lax.psum_scatter(partial_rows, 'tensor', scatter_dimension=0, tiled=True)]
    all_gather x1, waiting for transfers between devices: 19.2 us -> 0.02 us  [fetch_mixer(): lax.all_gather(w_query, 'fsdp', axis=0, tiled=True)]
    ppermute x0 -> x8, starting transfers between devices: none -> 16.3 us  [settle_surface_all(): ppermute(inter, axis_name, perm=list(map(lambda c: (c, c ^ local_next), r...]
  transfers between devices with their start and end apart: 25 -> 29, of which waited for: 19 -> 20; matrix products, arithmetic and copies ran while one was open for 36% -> 41% of each run, Pallas kernels for 0% -> 0%
where the time goes in v1:
time: 1480 us; the launch traced here: 1470 us
  waiting for transfers between devices  716 us (48%)
  matrix products  332 us (22%)
  other arithmetic  233 us (16%)
  local copies, waits for them, and re-layouts  75.7 us (5%)
  blocking collectives  72.4 us (5%)
  starting transfers between devices  17.9 us (1%)
  between operations  17.5 us (1%)
    reduce_scatter x4, waiting for transfers between devices, scatter_rows(): lax.psum_scatter(partial_rows, 'tensor', scatter_dimension=0, tiled=True)  225 us
    another operation x5, other arithmetic, delta_rule(): jax.scipy.linalg.solve_triangular(system, scaled_values, lower=True, unit...  160 us
    ppermute x8, waiting for transfers between devices, settle_surface_all(): ppermute(inter, axis_name, perm=list(map(lambda c: (c, c ^ local_next), r...  148 us
    all_gather x1, waiting for transfers between devices, fetch_ffn(): lax.all_gather(w_down, 'fsdp', axis=1, tiled=True)  67.2 us
    all_gather x1, waiting for transfers between devices, fetch_ffn(): lax.all_gather(w_up, 'fsdp', axis=0, tiled=True)  54.8 us
    dot_general x24, matrix products, advance(): jnp.einsum('hvk,htk->htv', memory, query_n, precision=lax.Precision.HIGHEST)  52.5 us
    dot_general x9, matrix products, matmul(): return jnp.dot(left, right, preferred_element_type=jnp.float32)  46.9 us
    dot_general x24, matrix products, advance(): jnp.einsum('htk,hvk->htv', solved_k, memory, precision=lax.Precision.HIGH...  46.2 us
  transfers between devices with their start and end apart: 29, of which 20 were waited for; matrix products, arithmetic and copies ran while one was open for 41% of the time, Pallas kernels for 0%

profile of v1, /device:TPU:0, one launch (start us, length us, event | category | flops | bytes accessed | tf_op | source)
XLA Modules:
  0.0 1465.4 jit_solution(4742324829644785677)
XLA Ops:
  36.9 39.0 %collective-permute-done.1 = bf16[256,2048]{1,0:T(8,128)(2,1)} collective-permute-done((bf16[256,2048]{1,0:T(8,128)(2,1)S(1)}, bf16[256,2048]{1,0:T(8,128)(2,1)}, u32[]{:S(2)}, u32[]{:S(2)}) %collective-permute-start.1) | collective-permute-done | bytes 1048608 | tf_op jit(solution)/shard_map/ppermute | solution.py:151
  97.0 18.1 %all-gather.9.cloned.1.call-done = bf16[2048,512]{1,0:T(8,128)(2,1)} async-done(((bf16[1024,512]{1,0:T(8,128)(2,1)}), bf16[2048,512]{1,0:T(8,128)(2,1)}) %all-gather.9.cloned.1.call-update) | async-done | bytes 2097168 | tf_op jit(solution)/shard_map/all_gather | solution.py:171
  132.4 158.4 %custom-call.12 = f32[8,4,1,64,64]{3,4,2,1,0:T(8,128)S(1)} custom-call(f32[8,4,1,64,64]{4,3,2,1,0:T(8,128)} %add_bitcast_fusion), custom_call_target="InvertDiagBlocksLowerTriangular" | custom-call | tf_op jit(solution)/shard_map/jvp(jit(_solve_triangular))/vmap(vmap())/triangular_solve | solution.py:57
  306.8 70.5 %while.48 = (s32[]{:T(128)}, f32[4,128,128]{2,1,0:T(8,128)S(1)}, f32[8,4,64,128]{3,2,1,0:T(8,128)}, f32[8,4,128,128]{3,2,1,0:T(8,128)}, f32[8,1,64,1]{2,3,1,0:T(...) while((s32[]{:T(128)}, f32[4,128,128]{2,1,0:T(8,128)S(1)}, ...), condition=%wide.region_5.7_spmd.clone, body=%wide.region_4.6_spmd.clone.sunk | while | flops 176717824 | bytes 3283676 | solution.py:85
  398.7 70.2 %reduce-scatter.16.cloned.1.call-done = f32[128,2048]{1,0:T(8,128)} async-done(((f32[512,2048]{1,0:T(8,128)}), f32[128,2048]{1,0:T(8,128)}) %reduce-scatter.16.cloned.1.call-update) | async-done | bytes 1048592 | tf_op jit(solution)/shard_map/reduce_scatter | solution.py:164
  472.2 12.2 collective-permute-done.2
  489.1 32.7 %collective-permute-done.4 = bf16[128,2048]{1,0:T(8,128)(2,1)S(1)} collective-permute-done((bf16[128,2048]{1,0:T(8,128)(2,1)S(1)}, bf16[128,2048]{1,0:T(8,128)(2,1)S(1)}, u32[]{:S(2)}, u32[]{:S(2)}) %collective-permute-start.4) | collective-permute-done | bytes 524320 | tf_op jit(solution)/shard_map/ppermute | solution.py:151
  525.0 20.5 %all-gather.19.cloned.1.call-done = bf16[2048,1408]{1,0:T(8,128)(2,1)} async-done(((bf16[1024,1408]{1,0:T(8,128)(2,1)}), bf16[2048,1408]{1,0:T(8,128)(2,1)}) %all-gather.19.cloned.1.call-update) | async-done | bytes 5767184 | tf_op jit(solution)/shard_map/all_gather | solution.py:182
  545.5 11.6 collective-permute-done.3
  566.9 54.8 %all-gather.21.cloned.1.call-done = bf16[2048,1408]{1,0:T(8,128)(2,1)} async-done(((bf16[1024,1408]{1,0:T(8,128)(2,1)}), bf16[2048,1408]{1,0:T(8,128)(2,1)}) %all-gather.21.cloned.1.call-update) | async-done | bytes 5767184 | tf_op jit(solution)/shard_map/all_gather | solution.py:183
  630.6 67.2 %all-gather.23.cloned.1.call-done = bf16[1408,2048]{1,0:T(8,128)(2,1)} async-done(((bf16[1408,1024]{1,0:T(8,128)(2,1)}), bf16[1408,2048]{1,0:T(8,128)(2,1)}) %all-gather.23.cloned.1.call-update) | async-done | bytes 5767184 | tf_op jit(solution)/shard_map/all_gather | solution.py:184
  738.7 58.8 %reduce-scatter.20.cloned.1.call-done = f32[128,2048]{1,0:T(8,128)} async-done(((f32[512,2048]{1,0:T(8,128)}), f32[128,2048]{1,0:T(8,128)}) %reduce-scatter.20.cloned.1.call-update) | async-done | bytes 1048592 | tf_op jit(solution)/shard_map/reduce_scatter | solution.py:164
  801.1 12.2 collective-permute-done.6
  830.9 31.7 %collective-permute-done.7 = bf16[256,2048]{1,0:T(8,128)(2,1)} collective-permute-done((bf16[256,2048]{1,0:T(8,128)(2,1)}, bf16[256,2048]{1,0:T(8,128)(2,1)}, u32[]{:S(2)}, u32[]{:S(2)}) %collective-permute-start.7) | collective-permute-done | bytes 1048608 | tf_op jit(solution)/shard_map/ppermute | solution.py:151
  882.4 125.5 %while.49 = (s32[]{:T(128)}, f32[4,128,128]{2,1,0:T(8,128)S(1)}, f32[8,4,64,128]{3,2,1,0:T(8,128)}, f32[8,4,64,128]{3,2,1,0:T(8,128)}, f32[8,4,64,64]{3,2,1,0:T(...) while((s32[]{:T(128)}, f32[4,128,128]{2,1,0:T(8,128)S(1)}, ...), condition=%wide.region_14.16_spmd.clone, body=%wide.region_13.15_spmd.clone.sunk | while | flops 352911360 | bytes 4731118 | solution.py:85
  1119.2 42.9 %reduce-scatter.26.cloned.1.call-done = bf16[256,512]{1,0:T(8,128)(2,1)} async-done(((bf16[2048,512]{1,0:T(8,128)(2,1)}), bf16[256,512]{1,0:T(8,128)(2,1)}) %reduce-scatter.26.cloned.1.call-update) | async-done | bytes 262160 | tf_op jit(solution)/shard_map/reduce_scatter | solution.py:323
  1164.0 42.5 %reduce-scatter.28.cloned.1.call-done = bf16[256,512]{1,0:T(8,128)(2,1)} async-done(((bf16[2048,512]{1,0:T(8,128)(2,1)}), bf16[256,512]{1,0:T(8,128)(2,1)}) %reduce-scatter.28.cloned.1.call-update) | async-done | bytes 262160 | tf_op jit(solution)/shard_map/reduce_scatter | solution.py:326
  1208.3 42.9 %reduce-scatter.30.cloned.1.call-done = bf16[256,512]{1,0:T(8,128)(2,1)} async-done(((bf16[2048,512]{1,0:T(8,128)(2,1)}), bf16[256,512]{1,0:T(8,128)(2,1)}) %reduce-scatter.30.cloned.1.call-update) | async-done | bytes 262160 | tf_op jit(solution)/shard_map/reduce_scatter | solution.py:329
  1253.1 42.8 %reduce-scatter.32.cloned.1.call-done = bf16[512,256]{1,0:T(8,128)(2,1)} async-done(((bf16[512,2048]{1,0:T(8,128)(2,1)}), bf16[512,256]{1,0:T(8,128)(2,1)}) %reduce-scatter.32.cloned.1.call-update) | async-done | bytes 262160 | tf_op jit(solution)/shard_map/reduce_scatter | solution.py:335
  1297.6 77.3 %reduce-scatter.22.cloned.1.call-done = f32[128,2048]{1,0:T(8,128)} async-done(((f32[512,2048]{1,0:T(8,128)}), f32[128,2048]{1,0:T(8,128)}) %reduce-scatter.22.cloned.1.call-update) | async-done | bytes 1048592 | tf_op jit(solution)/shard_map/reduce_scatter | solution.py:164
  1376.4 18.8 %all-reduce.36 = (bf16[2048]{0:T(1024)(128)(2,1)S(1)}, f32[128]{0:T(128)S(1)}, bf16[2048]{0:T(1024)(128)(2,1)S(1)}) all-reduce(f32[2048]{0:T(1024)S(1)} %get-tuple-element.717, f32[128]{0:T(128)S(1)} %copy-done.109, f32[2048]{0:T(1024)S(1)} %get-tuple-element.701), channel_id=1, replica_groups=mesh['dp'=4,'fsdp'=2,'tensor'=4] {'tensor'}, use_global_device_ids=true, to_apply=%region_23.26 | all-reduce | flops 4224 | bytes 25600 | tf_op jit(solution)/shard_map/psum | solution.py:312
  1395.2 14.7 %all-reduce.37 = (bf16[2048]{0:T(1024)(128)(2,1)S(1)}, bf16[2048]{0:T(1024)(128)(2,1)S(1)}) all-reduce(bf16[2048]{0:T(1024)(128)(2,1)S(1)} %get-tuple-element.791, bf16[2048]{0:T(1024)(128)(2,1)S(1)} %get-tuple-element.793), channel_id=6, replica_groups=mesh['dp'=4,'fsdp'=2,'tensor'=4] {'dp','fsdp'}, use_global_device_ids=true, to_apply=%region_24.27.clone | all-reduce | flops 4096 | bytes 16384
  1409.9 24.7 %all-reduce.35 = (f32[4,512]{1,0:T(4,128)}, f32[4,512]{1,0:T(4,128)}, f32[4,512]{1,0:T(4,128)}, f32[128]{0:T(128)}) all-reduce(f32[4,512]{1,0:T(4,128)S(1)} %pad_add_fusion.2, f32[4,512]{1,0:T(4,128)S(1)} %pad_add_fusion.1, f32[4,512]{1,0:T(4,128)S(1)} %pad_add_fusion, ...), channel_id=1, replica_groups=mesh['dp'=4,'fsdp'=2,'tensor'=4] {'dp','fsdp'}, use_global_device_ids=true, to_apply=%region_34.37 | all-reduce | flops 6272 | bytes 50176 | tf_op jit(solution)/shard_map/psum | solution.py:313
  1435.8 19.3 %reduce-scatter.18.cloned.1.call-done = f32[128,2048]{1,0:T(8,128)} async-done(((f32[512,2048]{1,0:T(8,128)}), f32[128,2048]{1,0:T(8,128)}) %reduce-scatter.18.cloned.1.call-update) | async-done | bytes 1048592 | tf_op jit(solution)/shard_map/reduce_scatter | solution.py:164
  (617 shorter events, 534.1 us)
Async XLA Ops:
  7.2 72.7 %all-gather.13.cloned.1.call-start = ((), (), s32[]{:S(2)}) async-start(), calls=%async_computation.15 | async-start | bytes 3145728 | tf_op jit(solution)/shard_map/all_gather | solution.py:170
  7.9 75.8 %all-gather.11.cloned.1.call-start = ((), (), s32[]{:S(2)}) async-start(), calls=%async_computation.14 | async-start | bytes 3145728 | tf_op jit(solution)/shard_map/all_gather | solution.py:172
  8.7 106.3 %all-gather.9.cloned.1.call-start = ((), (), s32[]{:S(2)}) async-start(), calls=%async_computation.13 | async-start | bytes 3145728 | tf_op jit(solution)/shard_map/all_gather | solution.py:171
  9.5 371.4 %all-gather.15.cloned.1.call-start = ((), (), s32[]{:S(2)}) async-start(), calls=%async_computation.16 | async-start | bytes 3145728 | tf_op jit(solution)/shard_map/all_gather | solution.py:173
  10.0 376.8 %all-gather.17.cloned.1.call-start = ((), (), s32[]{:S(2)}) async-start(), calls=%async_computation.17 | async-start | bytes 3145728 | tf_op jit(solution)/shard_map/all_gather | solution.py:175
  18.1 450.8 %reduce-scatter.16.cloned.1.call-start = ((), (), s32[]{:S(2)}) async-start(), calls=%async_computation.18 | async-start | bytes 5242880 | tf_op jit(solution)/shard_map/reduce_scatter | solution.py:164
  391.9 153.6 %all-gather.19.cloned.1.call-start = ((), (), s32[]{:S(2)}) async-start(), calls=%async_computation.19 | async-start | bytes 8650752 | tf_op jit(solution)/shard_map/all_gather | solution.py:182
  392.7 229.0 %all-gather.21.cloned.1.call-start = ((), (), s32[]{:S(2)}) async-start(), calls=%async_computation.20 | async-start | bytes 8650752 | tf_op jit(solution)/shard_map/all_gather | solution.py:183
  393.4 304.3 %all-gather.23.cloned.1.call-start = ((), (), s32[]{:S(2)}) async-start(), calls=%async_computation.21 | async-start | bytes 8650752 | tf_op jit(solution)/shard_map/all_gather | solution.py:184
  394.1 403.3 %reduce-scatter.20.cloned.1.call-start = ((), (), s32[]{:S(2)}) async-start(), calls=%async_computation.23 | async-start | bytes 5242880 | tf_op jit(solution)/shard_map/reduce_scatter | solution.py:164
  485.8 71.3 %collective-permute-start.3 = (bf16[256,2048]{1,0:T(8,128)(2,1)}, bf16[256,2048]{1,0:T(8,128)(2,1)}, u32[]{:S(2)}, u32[]{:S(2)}) collective-permute-start(bf16[256,2048]{1,0:T(8,128)(2,1)} %maximum_select_fusion.5), channel_id=1, source_target_pairs={{0,2},{1,3},{2,0},{3,1},{4,6},{5,7},{6,4},{7,5},{8,10},{9,11},{10,... | collective-permute-start | bytes 3145736 | tf_op jit(solution)/shard_map/ppermute | solution.py:151
  523.0 107.6 %collective-permute-start.5 = (bf16[256,2048]{1,0:T(8,128)(2,1)}, bf16[256,2048]{1,0:T(8,128)(2,1)}, u32[]{:S(2)}, u32[]{:S(2)}) collective-permute-start(bf16[256,2048]{1,0:T(8,128)(2,1)} %maximum_select_fusion.6), channel_id=1, source_target_pairs={{0,2},{1,3},{2,0},{3,1},{4,6},{5,7},{6,4},{7,5},{8,10},{9,11},{10,... | collective-permute-start | bytes 3145736 | tf_op jit(solution)/shard_map/ppermute | solution.py:151
  720.6 382.1 %reduce-scatter.34.cloned.1.call-start = ((), (), s32[]{:S(2)}) async-start(), calls=%async_computation.30 | async-start | bytes 6488064 | tf_op jit(solution)/shard_map/reduce_scatter | solution.py:341
  729.5 375.4 %reduce-scatter.36.cloned.1.call-start = ((), (), s32[]{:S(2)}) async-start(), calls=%async_computation.31 | async-start | bytes 6488064 | tf_op jit(solution)/shard_map/reduce_scatter | solution.py:344
  738.3 369.0 %reduce-scatter.38.cloned.1.call-start = ((), (), s32[]{:S(2)}) async-start(), calls=%async_computation.32 | async-start | bytes 6488064 | tf_op jit(solution)/shard_map/reduce_scatter | solution.py:347
  814.6 48.1 %collective-permute-start.7 = (bf16[256,2048]{1,0:T(8,128)(2,1)}, bf16[256,2048]{1,0:T(8,128)(2,1)}, u32[]{:S(2)}, u32[]{:S(2)}) collective-permute-start(bf16[256,2048]{1,0:T(8,128)(2,1)} %maximum_select_fusion.7), channel_id=1, source_target_pairs={{0,2},{1,3},{2,0},{3,1},{4,6},{5,7},{6,4},{7,5},{8,10},{9,11},{10,... | collective-permute-start | bytes 3145736 | tf_op jit(solution)/shard_map/ppermute | solution.py:151
  830.9 278.8 %reduce-scatter.40.cloned.1.call-start = ((), (), s32[]{:S(2)}) async-start(), calls=%async_computation.33 | async-start | bytes 589824
  1038.6 78.8 %reduce-scatter.24.cloned.1.call-start = ((), (), s32[]{:S(2)}) async-start(), calls=%async_computation.25 | async-start | bytes 2359296 | tf_op jit(solution)/shard_map/reduce_scatter | solution.py:320
  1055.9 106.3 %reduce-scatter.26.cloned.1.call-start = ((), (), s32[]{:S(2)}) async-start(), calls=%async_computation.26 | async-start | bytes 2359296 | tf_op jit(solution)/shard_map/reduce_scatter | solution.py:323
  1062.7 143.9 %reduce-scatter.28.cloned.1.call-start = ((), (), s32[]{:S(2)}) async-start(), calls=%async_computation.27 | async-start | bytes 2359296 | tf_op jit(solution)/shard_map/reduce_scatter | solution.py:326
  1069.5 181.8 %reduce-scatter.30.cloned.1.call-start = ((), (), s32[]{:S(2)}) async-start(), calls=%async_computation.28 | async-start | bytes 2359296 | tf_op jit(solution)/shard_map/reduce_scatter | solution.py:329
  1073.2 222.6 %reduce-scatter.32.cloned.1.call-start = ((), (), s32[]{:S(2)}) async-start(), calls=%async_computation.29 | async-start | bytes 2359296 | tf_op jit(solution)/shard_map/reduce_scatter | solution.py:335
  1079.3 295.6 %reduce-scatter.22.cloned.1.call-start = ((), (), s32[]{:S(2)}) async-start(), calls=%async_computation.24 | async-start | bytes 5242880 | tf_op jit(solution)/shard_map/reduce_scatter | solution.py:164
  1091.9 363.2 %reduce-scatter.18.cloned.1.call-start = ((), (), s32[]{:S(2)}) async-start(), calls=%async_computation.22 | async-start | bytes 5242880 | tf_op jit(solution)/shard_map/reduce_scatter | solution.py:164
  (124 other events, 4621.3 us)
Sparse Core Ops, SparseCore 0:
  9.6 35.9 all-gather.12
  47.2 33.1 all-gather.10
  81.9 33.1 all-gather.8
  116.4 33.2 all-gather.14
  151.1 33.2 all-gather.16
  392.0 76.8 reduce-scatter.15
  470.5 74.9 all-gather.18
  547.1 74.4 all-gather.20
  623.2 74.4 all-gather.22
  720.7 76.7 reduce-scatter.19
  800.9 59.5 reduce-scatter.33
  864.2 58.9 reduce-scatter.35
  926.7 59.0 reduce-scatter.37
  1038.8 34.2 reduce-scatter.39
  1076.2 41.1 reduce-scatter.23
  1120.9 41.2 reduce-scatter.25
  1165.3 41.1 reduce-scatter.27
  1210.0 41.2 reduce-scatter.29
  1254.6 41.2 reduce-scatter.31
  1298.1 76.7 reduce-scatter.21
  1377.2 77.8 reduce-scatter.17
